TPU v7x, 32 devices: a whole 2x2x4 slice. The times are simulated.
32 devices in a mesh: rep: 2 (over y), sample: 4 (over z), head: 4 (over x, core).
Axes of the slice: x: 2, y: 2, z: 4, core: 2. Of those that a mesh axis runs over, the one named last changes fastest.
Arguments:
- x_pre: bfloat16 [8, 128, 8192], P(('rep', 'sample'), None, 'head'), parts along dimension 0, may hold values from -120 to 120
- z_pre: bfloat16 [8, 128, 8192], P(('rep', 'sample'), None, 'head'), parts along dimension 0, may hold values from -6 to 6
- b_pre: bfloat16 [8, 128, 512], P(('rep', 'sample')), parts along dimension 0, may hold values from -1.796875 to 1.796875
- c_pre: bfloat16 [8, 128, 512], P(('rep', 'sample')), parts along dimension 0, may hold values from -0.5390625 to 0.5390625
- dt_pre: float32 [8, 128, 128], P(('rep', 'sample'), None, 'head'), parts along dimension 0, may hold values from -1.5 to 7.5
- lengths: int32 [8], P(('rep', 'sample')), parts along dimension 0, may hold values from 64 to 128, as said below
- init_state: float32 [8, 128, 8192], P(('rep', 'sample'), None, 'head'), parts along dimension 0, may hold values from -6 to 6
- a_rates: float32 [128], P('head'), may hold values from 0.005 to 0.3
- dt_bias: float32 [128], P('head'), may hold values from -2 to -1
- skip_scale: float32 [128], P('head'), may hold values from 0.5 to 2
- norm_gain: float32 [8192], P('head'), may hold values from 0.5 to 1.5
- x_dec: bfloat16 [8, 4, 8192], P(('rep', 'sample'), None, 'head'), parts along dimension 0, may hold values from -120 to 120
- z_dec: bfloat16 [8, 4, 8192], P(('rep', 'sample'), None, 'head'), parts along dimension 0, may hold values from -6 to 6
- b_dec: bfloat16 [8, 4, 512], P(('rep', 'sample')), parts along dimension 0, may hold values from -6 to 6
- c_dec: bfloat16 [8, 4, 512], P(('rep', 'sample')), parts along dimension 0, may hold values from -0.5390625 to 0.5390625
- dt_dec: float32 [8, 4, 128], P(('rep', 'sample'), None, 'head'), parts along dimension 0, may hold values from -3 to 3
Outputs:
- out_pre: bfloat16 [8, 128, 8192], P(('rep', 'sample'), None, 'head'), parts along dimension 0
- final_state: bfloat16 [8, 128, 8192], P(('rep', 'sample'), None, 'head'), parts along dimension 0
- out_dec: bfloat16 [8, 4, 8192], P(('rep', 'sample'), None, 'head'), parts along dimension 0
There are 2 independent parts, one for each index of `rep`. A program takes and returns all parts, laid end to end along the dimension named above; an argument that names none is the same for every part. Nothing has to cross between parts.
Inputs may be any that keep to these rules, and one draw needn't show every extreme that they name: Each prompt's valid tokens are the first lengths[p] of its 128 positions; some prompt uses all 128.
All inputs are finite; a program needn't handle non-finite values.
Results may differ from a plain program's by a relative error of at most 0.006.
Values may be sent and summed in bfloat16 or wider, within the bound.
No kernel may reach another device: no remote copies, remote signals or barrier semaphores. Data moves between devices by JAX's collectives and lax.ppermute only.
A program may use at most 64 MiB of HBM per device.

v0:
```python
import jax
import jax.numpy as jnp
from jax import lax
from jax.sharding import PartitionSpec as P

H = 128
P_SIZE = 64
G = 4
BLOCK = 128
epsilon = 1e-05
highest = lax.Precision.HIGHEST


def group_owners(first_head, head_count):
    head_ids = first_head + jnp.arange(head_count, dtype=jnp.int32)
    return head_ids // (H // G)


def group_pick(owners):
    return (owners[:, None] == jnp.arange(G, dtype=jnp.int32)[None, :]).astype(jnp.float32)


def scan_prompt(inputs, b_rows, c_rows, step_delta, rates, skip_gain, start_state, owners):
    length = inputs.shape[0]
    head_count = step_delta.shape[1]
    head_width = inputs.shape[1] // head_count
    states = b_rows.shape[1] // G
    blocks = length // BLOCK
    b_groups = b_rows.reshape(blocks, BLOCK, G, states)
    c_groups = c_rows.reshape(blocks, BLOCK, G, states)
    group_scores = jnp.einsum(
        "cign,cjgn->cijg", c_groups, b_groups, preferred_element_type=jnp.float32
    )
    head_scores = jnp.take(group_scores, owners, axis=3)
    b_head = jnp.take(b_groups, owners, axis=2).astype(jnp.float32)
    c_head = jnp.take(c_groups, owners, axis=2).astype(jnp.float32)
    values = inputs.astype(jnp.float32).reshape(blocks, BLOCK, head_count, head_width)
    block_delta = step_delta.reshape(blocks, BLOCK, head_count)
    decays = jnp.cumsum(-block_delta * rates, axis=1)
    causal_mask = (jnp.arange(BLOCK)[:, None] >= jnp.arange(BLOCK)[None, :])[None, :, :, None]
    spread = decays[:, :, None, :] - decays[:, None, :, :]
    weights = jnp.where(causal_mask, jnp.exp(jnp.where(causal_mask, spread, 0.0)), 0.0)
    scores = head_scores * weights * block_delta[:, None, :, :]
    inner_part = jnp.einsum("cijh,cjhp->cihp", scores, values, precision=highest)
    tail_decay = jnp.exp(decays[:, -1:, :] - decays) * block_delta
    block_states = jnp.einsum(
        "cjhn,cjhp->cnhp", b_head * tail_decay[..., None], values, precision=highest
    )
    block_totals = jnp.exp(decays[:, -1, :])

    def carry_step(carried, pieces):
        factor, fresh_term = pieces
        return (factor[None, :, None] * carried + fresh_term, carried)

    final_carry, starts = lax.scan(
        carry_step,
        start_state.reshape(states, head_count, head_width),
        (block_totals, block_states),
    )
    outer_part = (
        jnp.einsum("cihn,cnhp->cihp", c_head, starts, precision=highest)
        * jnp.exp(decays)[..., None]
    )
    result = inner_part + outer_part + skip_gain[None, None, :, None] * values
    return (
        result.reshape(length, head_count * head_width),
        final_carry.reshape(states, head_count * head_width),
    )


def gate_values(result, gate_rows):
    gate_rows = gate_rows.astype(jnp.float32)
    return result * gate_rows * jax.nn.sigmoid(gate_rows)


def select_heads(c_rows, owners):
    shape_front = c_rows.shape[:2]
    states = c_rows.shape[2] // G
    grouped = c_rows.reshape(shape_front[0], shape_front[1], G, states)
    return jnp.take(grouped, owners, axis=2)


def body(
    x_pre,
    z_pre,
    b_pre,
    c_pre,
    dt_pre,
    lengths,
    init_state,
    a_rates,
    dt_bias,
    skip_scale,
    norm_gain,
    x_dec,
    z_dec,
    b_dec,
    c_dec,
    dt_dec,
):
    heads_here = a_rates.shape[0]
    head_width = x_pre.shape[2] // heads_here
    first_head = lax.axis_index("head") * heads_here
    owners = group_owners(first_head, heads_here)
    picker = group_pick(owners)
    length = x_pre.shape[1]
    positions = jnp.arange(length, dtype=jnp.int32)
    valid_mask = (positions[None, :] < lengths[:, None]).astype(jnp.float32)
    step_delta = jax.nn.softplus(dt_pre + dt_bias) * valid_mask[:, :, None]

    def one_prompt(pieces):
        inputs, b_rows, c_rows, prompt_delta, start_state = pieces
        return scan_prompt(
            inputs, b_rows, c_rows, prompt_delta, a_rates, skip_scale, start_state, owners
        )

    result, final_carry = lax.map(one_prompt, (x_pre, b_pre, c_pre, step_delta, init_state))
    final_state = final_carry.astype(jnp.bfloat16)
    gated_rows = gate_values(result, z_pre)
    pre_totals = lax.psum(jnp.sum(gated_rows * gated_rows, axis=-1), "head")
    norm_scale = lax.rsqrt(pre_totals[:, :, None] / (H * P_SIZE) + epsilon)
    out_pre = (gated_rows * norm_scale * norm_gain * valid_mask[:, :, None]).astype(jnp.bfloat16)
    slots_here = x_dec.shape[0]
    prompt_count = x_dec.shape[1]
    prompts_here = final_state.shape[0]
    states = final_state.shape[1]
    cached = final_state.reshape(prompts_here, states, heads_here, head_width)
    queries = lax.all_to_all(c_dec, "sample", split_axis=1, concat_axis=0, tiled=True)
    c_head = select_heads(queries, owners)
    answers = jnp.einsum("sphn,pnhq->sphq", c_head, cached, preferred_element_type=jnp.float32)
    answers = answers.reshape(answers.shape[0], prompts_here, heads_here * head_width)
    state_reads = lax.all_to_all(
        answers.astype(jnp.bfloat16), "sample", split_axis=0, concat_axis=1, tiled=True
    ).astype(answers.dtype)
    state_reads = state_reads.reshape(slots_here, prompt_count, heads_here, head_width)
    c_groups = c_dec.astype(jnp.float32).reshape(slots_here, prompt_count, G, states)
    b_groups = b_dec.astype(jnp.float32).reshape(slots_here, prompt_count, G, states)
    cb_dot = jnp.einsum("spgn,spgn->spg", c_groups, b_groups, precision=highest)
    cb_dot = jnp.einsum("spg,hg->sph", cb_dot, picker, precision=highest)
    step_sizes = jax.nn.softplus(dt_dec + dt_bias)
    decay_rate = jnp.exp(-step_sizes * a_rates)
    values = x_dec.astype(jnp.float32).reshape(slots_here, prompt_count, heads_here, head_width)
    fresh_term = (
        decay_rate[..., None] * state_reads + (step_sizes * cb_dot + skip_scale)[..., None] * values
    )
    gated_dec = gate_values(
        fresh_term.reshape(slots_here, prompt_count, heads_here * head_width), z_dec
    )
    dec_totals = lax.psum(jnp.sum(gated_dec * gated_dec, axis=-1), "head")
    dec_scale = lax.rsqrt(dec_totals[:, :, None] / (H * P_SIZE) + epsilon)
    out_dec = (gated_dec * dec_scale * norm_gain).astype(jnp.bfloat16)
    return (out_pre, final_state, out_dec)


def solution(mesh):
    in_specs = (
        P(("rep", "sample"), None, "head"),
        P(("rep", "sample"), None, "head"),
        P(("rep", "sample"), None, None),
        P(("rep", "sample"), None, None),
        P(("rep", "sample"), None, "head"),
        P(("rep", "sample")),
        P(("rep", "sample"), None, "head"),
        P("head"),
        P("head"),
        P("head"),
        P("head"),
        P(("rep", "sample"), None, "head"),
        P(("rep", "sample"), None, "head"),
        P(("rep", "sample"), None, None),
        P(("rep", "sample"), None, None),
        P(("rep", "sample"), None, "head"),
    )
    out_specs = (
        P(("rep", "sample"), None, "head"),
        P(("rep", "sample"), None, "head"),
        P(("rep", "sample"), None, "head"),
    )
    return jax.shard_map(body, mesh=mesh, in_specs=in_specs, out_specs=out_specs, check_vma=False)
```

profile of v0, /device:TPU:0, one launch (start us, length us, event | category | flops | bytes accessed | tf_op | source)
XLA Modules:
  0.0 61.4 jit_solution(16359119723385610459)
XLA Ops:
  0.7 0.8 %copy.168 = bf16[1,4,512]{2,0,1:T(2,128)(2,1)S(1)} copy(bf16[1,4,512]{2,1,0:T(4,128)(2,1)} %param.32) | data formatting | bytes 8192 | tf_op args[14]
  1.4 0.5 broadcast.360
  1.9 0.7 %reduce.6 = bf16[4,512]{1,0:T(4,128)(2,1)S(1)} reduce(bf16[4,1,512]{2,1,0:T(2,128)(2,1)S(1)} %bitcast.142, bf16[]{:T(256)} %broadcast.360), dimensions={1}, to_apply=%bitcast.126.reduce_sub_computation | reduce | bytes 8194
  2.6 0.6 reshape.510
  3.2 6.3 %all-to-all-start = ((bf16[4,2,256]{2,1,0:T(2,128)(2,1)}), bf16[4,2,256]{2,1,0:T(2,128)(2,1)}, u32[]{:S(2)}, u32[]{:S(2)}) async-start(bf16[4,2,256]{2,1,0:T(2,128)(2,1)} %reshape.510), calls=%async_computation | async-start | bytes 8192 | tf_op jit(solution)/shard_map/all_to_all | solution.py:128
  10.2 0.8 %negate_multiply_fusion = f32[1,128,32]{1,2,0:T(8,128)S(1)} fusion(f32[32]{0:T(128)} %param.25, f32[128]{0:T(128)S(1)} %compare_convert_fusion, f32[1,128,32]{1,2,0:T(8,128)} %param.22, f32[32]{0:T(128)} %param.26), kind=kLoop, calls=%fused_computation.73 | loop fusion | flops 40960 | bytes 33536 | tf_op jit(solution)/shard_map/while/body/eval_jaxpr/mul | solution.py:39
  11.1 0.2 reduce_window_sum.12
  11.4 0.6 compare_and_fusion
  11.9 0.6 iota_compare_fusion
  12.6 0.6 compare_select_fusion.3
  13.2 0.9 %reshape.439 = bf16[128,4,128]{2,1,0:T(4,128)(2,1)S(1)} reshape(bf16[1,128,512]{2,1,0:T(8,128)(2,1)} %param.21) | data formatting | bytes 262144 | tf_op jit(solution)/shard_map/reshape.21
  14.1 1.0 %copy.129 = bf16[1,128,512]{1,2,0:T(8,128)(2,1)S(1)} copy(bf16[1,128,512]{2,1,0:T(8,128)(2,1)} %param.21) | data formatting | bytes 262144 | tf_op args[3]
  15.2 2.0 %copy.127 = bf16[1,128,2048]{1,2,0:T(8,128)(2,1)} copy(bf16[1,128,2048]{2,1,0:T(8,128)(2,1)} %param.18) | data formatting | bytes 1048576 | tf_op args[0]
  17.2 1.2 %copy.133 = f32[1,128,2048]{1,2,0:T(8,128)} copy(bf16[1,128,2048]{2,1,0:T(8,128)(2,1)S(1)} %copy-done.2) | data formatting | bytes 1572864 | tf_op jit(solution)/shard_map/while/body/eval_jaxpr/convert_element_type | solution.py:37
  18.4 0.8 %copy.136 = bf16[1,128,512]{1,2,0:T(8,128)(2,1)} copy(bf16[1,128,512]{2,1,0:T(8,128)(2,1)S(1)} %copy-done.6) | data formatting | bytes 262144 | tf_op args[2]
  19.2 0.5 fusion.59
  19.7 0.6 reshape.449
  20.3 0.7 %copy.125 = f32[128,32]{0,1:T(8,128)} copy(f32[128,32]{1,0:T(8,128)S(1)} %bitcast.135) | data formatting | bytes 32768 | tf_op jit(solution)/shard_map/while/body/eval_jaxpr/sub | solution.py:41
  21.0 0.6 pad_clamp_fusion.1
  21.7 0.6 pad_clamp_fusion
  22.3 0.1 copy.130
  22.4 0.3 copy.131
  22.8 0.7 %multiply_bitcast_fusion = (f32[128,32]{0,1:T(8,128)}, f32[128,32]{0,1:T(8,128)}) fusion(f32[1,128,32]{1,2,0:T(8,128)S(1)} %copy.138, f32[32]{0:T(128)S(1)} %slice_bitcast_fusion, f32[128]{0:T(128)S(1)} %compare_convert_fusion, f32[1,128,32]{1,2,0:T(8,128)S(1)} %copy-done.8, f32[32]{0:T(128)S(1)} %copy-done.18), kind=kLoop, calls=%fused_computation.72 | loop fusion | flops 40960 | bytes 66304 | tf_op jit(solution)/shard_map/while/body/eval_jaxpr/mul | solution.py:47
  23.5 0.2 convolution_bitcast_fusion.1
  23.7 0.8 %gather_fusion = f32[32,128,128]{1,2,0:T(8,128)S(1)} fusion(f32[128,128,4]{0,1,2:T(8,128)S(1)} %convolution_bitcast_fusion.1, s32[1024]{0:T(1024)} %pad_clamp_fusion.1), kind=kCustom, calls=%fused_computation.2 | custom fusion | bytes 4194432 | tf_op jit(solution)/shard_map/while/body/eval_jaxpr/jit(_take)/gather | solution.py:34
  24.5 1.9 %gather_fusion.2 = bf16[32,128,128]{2,1,0:T(8,128)(2,1)} fusion(bf16[128,4,128]{2,0,1:T(8,128)(2,1)S(1)} %bitcast.129, s32[1024]{0:T(1024)} %pad_clamp_fusion), kind=kCustom, calls=%fused_computation.clone | custom fusion | bytes 2097280 | tf_op jit(solution)/shard_map/while/body/eval_jaxpr/jit(_take)/gather | solution.py:36
  26.5 4.0 %fusion.12 = f32[1,128,32,64]{1,3,2,0:T(8,128)S(1)} fusion(bf16[128,32,64]{0,2,1:T(8,128)(2,1)} %bitcast.137, f32[32,128,128]{1,2,0:T(8,128)S(1)} %gather_fusion, f32[128,32]{0,1:T(8,128)S(1)} %copy-done.17, f32[128,32]{0,1:T(8,128)S(1)} %copy-done.12, pred[32]{0:T(512)(128)(4,1)S(1)} %copy-done.26, pred[128,128]{0,1:T(8,128)(4,1)S(1)} %copy-done.14), kind=kOutput, calls=%fused_computation.16 | convolution fusion | flops 405798912 | bytes 3719200 | tf_op jit(solution)/shard_map/while/body/eval_jaxpr/cijh,cjhp->cihp/dot_general | solution.py:44
  30.5 2.2 %fusion.17 = f32[1,128,32,64]{1,3,2,0:T(8,128)S(1)} fusion(f32[1,128,32,64]{1,3,2,0:T(8,128)S(1)} %fusion.12, f32[128,32,64]{0,2,1:T(8,128)S(1)} %bitcast.131, bf16[32,128,128]{2,1,0:T(8,128)(2,1)S(1)} %copy-done, f32[1,128,32,64]{1,3,2,0:T(8,128)S(1)} %bitcast.132, pred[32]{0:T(512)(128)(4,1)S(1)} %copy-done.26, f32[32]{0:T(128)S(1)} %copy-done.25, ...), kind=kOutput, calls=%fused_computation.20 | convolution fusion | flops 404226048 | bytes 5259424 | tf_op jit(solution)/shard_map/while/body/eval_jaxpr/cihn,cnhp->cihp/dot_general | solution.py:61
  32.8 0.3 copy.134
  33.2 0.5 copy-done.7
  33.6 0.1 copy.137
  33.8 1.8 %gather_fusion.3 = bf16[32,128,128]{2,1,0:T(8,128)(2,1)} fusion(bf16[128,4,128]{2,0,1:T(8,128)(2,1)S(1)} %bitcast.130, s32[1024]{0:T(1024)} %pad_clamp_fusion), kind=kCustom, calls=%fused_computation.1.clone | custom fusion | bytes 2097280 | tf_op jit(solution)/shard_map/while/body/eval_jaxpr/jit(_take)/gather | solution.py:35
  35.8 0.4 multiply_reduce_fusion
  36.2 2.7 %fusion = f32[32,128,64]{1,2,0:T(8,128)S(1)} fusion(bf16[128,32,64]{0,2,1:T(8,128)(2,1)S(1)} %bitcast.138, bf16[32,128,128]{2,1,0:T(8,128)(2,1)} %gather_fusion.3, f32[128,32]{0,1:T(8,128)S(1)} %copy-done.16, pred[32]{0:T(512)(128)(4,1)S(1)} %copy-done.27), kind=kOutput, calls=%fused_computation.4 | convolution fusion | flops 404226048 | bytes 2637856 | tf_op jit(solution)/shard_map/while/body/eval_jaxpr/cjhn,cjhp->cnhp/dot_general | solution.py:46
  39.0 0.4 fusion.26
  39.5 0.7 %reshape.511 = bf16[4,1,512]{2,1,0:T(2,128)(2,1)S(1)} reshape(bf16[4,2,256]{2,1,0:T(2,128)(2,1)} %all-to-all-done) | data formatting | bytes 8192
  40.2 0.7 %gather_fusion.1 = bf16[32,4,128]{2,1,0:T(4,128)(2,1)S(1)} fusion(bf16[4,4,128]{2,0,1:T(4,128)(2,1)S(1)} %bitcast.141, s32[1024]{0:T(1024)} %pad_clamp_fusion.1), kind=kCustom, calls=%fused_computation.3 | custom fusion | bytes 65664 | tf_op jit(solution)/shard_map/jit(_take)/gather | solution.py:80
  41.0 0.4 fusion.18
  41.5 0.7 %reduce.7 = bf16[4,2048]{1,0:T(4,128)(2,1)S(1)} reduce(bf16[4,1,2048]{2,1,0:T(2,128)(2,1)S(1)} %convert_element_type.108, bf16[]{:T(256)} %broadcast.360), dimensions={1}, to_apply=%convert_element_type.108.reduce_sub_computation | reduce | bytes 32770 | tf_op jit(solution)/shard_map/convert_element_type | solution.py:133
  42.2 0.6 %reshape.512 = bf16[4,2,1024]{2,1,0:T(2,128)(2,1)} reshape(bf16[4,2048]{1,0:T(4,128)(2,1)S(1)} %reduce.7) | data formatting | bytes 32768
  42.8 5.1 %all-to-all-start.1 = ((bf16[4,2,1024]{2,1,0:T(2,128)(2,1)}), bf16[4,2,1024]{2,1,0:T(2,128)(2,1)S(1)}, u32[]{:S(2)}, u32[]{:S(2)}) async-start(bf16[4,2,1024]{2,1,0:T(2,128)(2,1)} %reshape.512), calls=%async_computation.1 | async-start | bytes 32768 | tf_op jit(solution)/shard_map/all_to_all | solution.py:132
  47.9 0.2 fusion.21
  48.1 1.0 %copy.145 = bf16[1,128,2048]{2,1,0:T(8,128)(2,1)} copy(bf16[1,128,2048]{1,2,0:T(8,128)(2,1)S(1)} %fusion.26) | data formatting | bytes 1048576
  49.5 4.0 %all-to-all-done.1 = bf16[4,2,1024]{2,1,0:T(2,128)(2,1)S(1)} async-done(((bf16[4,2,1024]{2,1,0:T(2,128)(2,1)}), bf16[4,2,1024]{2,1,0:T(2,128)(2,1)S(1)}, u32[]{:S(2)}, u32[]{:S(2)}) %all-to-all-start.1) | async-done | bytes 16416 | tf_op jit(solution)/shard_map/all_to_all | solution.py:132
  53.6 0.2 multiply_reduce_fusion.1
  53.8 5.6 %all-reduce = (f32[1,128]{1,0:T(1,128)S(1)}, f32[1,4]{1,0:T(1,128)S(1)}) all-reduce(f32[1,128]{1,0:T(1,128)S(1)} %bitcast.143, f32[1,4]{1,0:T(1,128)S(1)} %bitcast.144), channel_id=1, replica_groups=mesh['rep'=2,'sample'=4,'head'=4] {'head'}, use_global_device_ids=true, to_apply=%region_2.4 | all-reduce | flops 132 | bytes 1056 | tf_op jit(solution)/shard_map/psum | solution.py:120
  59.6 0.6 %copy.146 = bf16[1,4,2048]{2,1,0:T(4,128)(2,1)} copy(bf16[1,4,2048]{2,0,1:T(2,128)(2,1)S(1)} %multiply_convert_fusion.1) | data formatting | bytes 32768
  60.2 1.2 %multiply_convert_fusion = bf16[1,128,2048]{2,1,0:T(8,128)(2,1)} fusion(f32[128]{0:T(128)S(1)} %copy-done.21, f32[2048]{0:T(1024)S(1)} %copy-done.9, f32[128]{0:T(128)S(1)} %rsqrt_bitcast_fusion.1, f32[1,128,2048]{2,1,0:T(8,128)S(1)} %copy.134, bf16[1,128,2048]{2,1,0:T(8,128)(2,1)S(1)} %copy-done.3), kind=kLoop, calls=%fused_computation.41 | loop fusion | flops 2621440 | bytes 2106368 | tf_op jit(solution)/shard_map/convert_element_type | solution.py:122
  (84 shorter events, 1.3 us)
Async XLA Ops:
  0.6 16.6 %copy-start.2 = (bf16[1,128,2048]{2,1,0:T(8,128)(2,1)S(1)}, bf16[1,128,2048]{2,1,0:T(8,128)(2,1)}, u32[]{:S(2)}) copy-start(bf16[1,128,2048]{2,1,0:T(8,128)(2,1)} %param.18) | copy-start | bytes 1572868
  0.6 17.8 %copy-start.6 = (bf16[1,128,512]{2,1,0:T(8,128)(2,1)S(1)}, bf16[1,128,512]{2,1,0:T(8,128)(2,1)}, u32[]{:S(2)}) copy-start(bf16[1,128,512]{2,1,0:T(8,128)(2,1)} %param.20) | copy-start | bytes 393220
  1.9 17.8 %copy-start.13 = (bf16[1,4,512]{2,1,0:T(4,128)(2,1)S(1)}, bf16[1,4,512]{2,1,0:T(4,128)(2,1)}, u32[]{:S(2)}) copy-start(bf16[1,4,512]{2,1,0:T(4,128)(2,1)} %param.32) | copy-start | bytes 12292
  3.2 36.3 %all-to-all-start = ((bf16[4,2,256]{2,1,0:T(2,128)(2,1)}), bf16[4,2,256]{2,1,0:T(2,128)(2,1)}, u32[]{:S(2)}, u32[]{:S(2)}) async-start(bf16[4,2,256]{2,1,0:T(2,128)(2,1)} %reshape.510), calls=%async_computation | async-start | bytes 8192 | tf_op jit(solution)/shard_map/all_to_all | solution.py:128
  10.2 12.5 %copy-start.20 = (f32[128]{0:T(128)}, f32[128]{0:T(128)S(1)}, u32[]{:S(2)}) copy-start(f32[128]{0:T(128)S(1)} %compare_convert_fusion) | copy-start | bytes 1540
  12.6 9.8 %copy-start.4 = (f32[1,128,2048]{2,1,0:T(8,128)S(1)}, f32[1,128,2048]{2,1,0:T(8,128)}, u32[]{:S(2)}) copy-start(f32[1,128,2048]{2,1,0:T(8,128)} %param.24) | copy-start | bytes 3145732
  17.2 5.6 %copy-start.8 = (f32[1,128,32]{1,2,0:T(8,128)S(1)}, f32[1,128,32]{1,2,0:T(8,128)}, u32[]{:S(2)}) copy-start(f32[1,128,32]{1,2,0:T(8,128)} %param.22) | copy-start | bytes 49156
  17.2 5.6 %copy-start.18 = (f32[32]{0:T(128)S(1)}, f32[32]{0:T(128)}, u32[]{:S(2)}) copy-start(f32[32]{0:T(128)} %param.26) | copy-start | bytes 388
  24.5 2.0 %copy-start.12 = (f32[128,32]{0,1:T(8,128)S(1)}, f32[128,32]{0,1:T(8,128)}, u32[]{:S(2)}) copy-start(f32[128,32]{0,1:T(8,128)} %copy.125) | copy-start | bytes 49156
  24.5 2.0 %copy-start.14 = (pred[128,128]{0,1:T(8,128)(4,1)S(1)}, pred[128,128]{0,1:T(8,128)(4,1)}, u32[]{:S(2)}) copy-start(pred[128,128]{0,1:T(8,128)(4,1)} %iota_compare_fusion) | copy-start | bytes 49156
  24.5 2.0 %copy-start.17 = (f32[128,32]{0,1:T(8,128)S(1)}, f32[128,32]{0,1:T(8,128)}, u32[]{:S(2)}) copy-start(f32[128,32]{0,1:T(8,128)} %get-tuple-element.77) | copy-start | bytes 49156
  24.5 2.0 %copy-start.26 = (pred[32]{0:T(512)(128)(4,1)S(1)}, pred[32]{0:T(512)(128)(4,1)}, u32[]{:S(2)}) copy-start(pred[32]{0:T(512)(128)(4,1)} %compare_and_fusion) | copy-start | bytes 100
  26.5 4.0 %copy-start = (bf16[32,128,128]{2,1,0:T(8,128)(2,1)S(1)}, bf16[32,128,128]{2,1,0:T(8,128)(2,1)}, u32[]{:S(2)}) copy-start(bf16[32,128,128]{2,1,0:T(8,128)(2,1)} %gather_fusion.2) | copy-start | bytes 3145732
  26.5 4.0 %copy-start.1 = (f32[1,128,2048]{1,2,0:T(8,128)S(1)}, f32[1,128,2048]{1,2,0:T(8,128)}, u32[]{:S(2)}) copy-start(f32[1,128,2048]{1,2,0:T(8,128)} %copy.133) | copy-start | bytes 3145732
  26.5 4.0 %copy-start.25 = (f32[32]{0:T(128)S(1)}, f32[32]{0:T(128)}, u32[]{:S(2)}) copy-start(f32[32]{0:T(128)} %param.27) | copy-start | bytes 388
  32.7 0.9 %copy-start.7 = (bf16[1,128,512]{1,2,0:T(8,128)(2,1)S(1)}, bf16[1,128,512]{1,2,0:T(8,128)(2,1)}, u32[]{:S(2)}) copy-start(bf16[1,128,512]{1,2,0:T(8,128)(2,1)} %copy.136) | copy-start | bytes 393220
  32.7 2.8 %copy-start.28 = (f32[32]{0:T(128)S(1)}, f32[32]{0:T(128)}, u32[]{:S(2)}) copy-start(f32[32]{0:T(128)} %fusion.59) | copy-start | bytes 388
  32.8 3.0 %copy-start.22 = (bf16[1,4,512]{2,1,0:T(4,128)(2,1)S(1)}, bf16[1,4,512]{2,1,0:T(4,128)(2,1)}, u32[]{:S(2)}) copy-start(bf16[1,4,512]{2,1,0:T(4,128)(2,1)} %param.31) | copy-start | bytes 12292
  32.8 3.0 %copy-start.19 = (f32[32]{0:T(128)S(1)}, f32[32]{0:T(128)}, u32[]{:S(2)}) copy-start(f32[32]{0:T(128)} %param.26) | copy-start | bytes 388
  32.8 3.0 %copy-start.23 = (f32[32]{0:T(128)S(1)}, f32[32]{0:T(128)}, u32[]{:S(2)}) copy-start(f32[32]{0:T(128)} %param.25) | copy-start | bytes 388
  32.8 2.9 %copy-start.24 = (f32[1,4,32]{2,1,0:T(4,128)S(1)}, f32[1,4,32]{2,1,0:T(4,128)}, u32[]{:S(2)}) copy-start(f32[1,4,32]{2,1,0:T(4,128)} %param.33) | copy-start | bytes 1540
  33.1 2.6 %copy-start.3 = (bf16[1,128,2048]{2,1,0:T(8,128)(2,1)S(1)}, bf16[1,128,2048]{2,1,0:T(8,128)(2,1)}, u32[]{:S(2)}) copy-start(bf16[1,128,2048]{2,1,0:T(8,128)(2,1)} %param.19) | copy-start | bytes 1572868
  33.2 3.0 %copy-start.5 = (bf16[1,128,2048]{1,2,0:T(8,128)(2,1)S(1)}, bf16[1,128,2048]{1,2,0:T(8,128)(2,1)}, u32[]{:S(2)}) copy-start(bf16[1,128,2048]{1,2,0:T(8,128)(2,1)} %copy.127) | copy-start | bytes 1572868
  33.2 3.0 %copy-start.16 = (f32[128,32]{0,1:T(8,128)S(1)}, f32[128,32]{0,1:T(8,128)}, u32[]{:S(2)}) copy-start(f32[128,32]{0,1:T(8,128)} %get-tuple-element.76) | copy-start | bytes 49156
  33.2 3.0 %copy-start.27 = (pred[32]{0:T(512)(128)(4,1)S(1)}, pred[32]{0:T(512)(128)(4,1)}, u32[]{:S(2)}) copy-start(pred[32]{0:T(512)(128)(4,1)} %compare_and_fusion) | copy-start | bytes 100
  36.2 3.2 %copy-start.15 = (bf16[4,4,128]{2,1,0:T(4,128)(2,1)S(1)}, bf16[4,4,128]{2,1,0:T(4,128)(2,1)}, u32[]{:S(2)}) copy-start(bf16[4,4,128]{2,1,0:T(4,128)(2,1)} %reshape.449) | copy-start | bytes 12292
  39.0 9.0 %copy-start.29 = (s32[32]{0:T(128)S(1)}, s32[32]{0:T(128)}, u32[]{:S(2)}) copy-start(s32[32]{0:T(128)} %get-tuple-element.79) | copy-start | bytes 388
  39.0 14.6 %copy-start.10 = (bf16[1,4,2048]{2,1,0:T(4,128)(2,1)S(1)}, bf16[1,4,2048]{2,1,0:T(4,128)(2,1)}, u32[]{:S(2)}) copy-start(bf16[1,4,2048]{2,1,0:T(4,128)(2,1)} %param.30) | copy-start | bytes 49156
  39.0 14.6 %copy-start.11 = (bf16[1,4,2048]{2,1,0:T(4,128)(2,1)S(1)}, bf16[1,4,2048]{2,1,0:T(4,128)(2,1)}, u32[]{:S(2)}) copy-start(bf16[1,4,2048]{2,1,0:T(4,128)(2,1)} %param.29) | copy-start | bytes 49156
  39.0 20.5 %copy-start.9 = (f32[2048]{0:T(1024)S(1)}, f32[2048]{0:T(1024)}, u32[]{:S(2)}) copy-start(f32[2048]{0:T(1024)} %param.28) | copy-start | bytes 24580
  39.0 21.2 %copy-start.21 = (f32[128]{0:T(128)S(1)}, f32[128]{0:T(128)}, u32[]{:S(2)}) copy-start(f32[128]{0:T(128)} %copy-done.20) | copy-start | bytes 1540
  42.8 10.7 %all-to-all-start.1 = ((bf16[4,2,1024]{2,1,0:T(2,128)(2,1)}), bf16[4,2,1024]{2,1,0:T(2,128)(2,1)S(1)}, u32[]{:S(2)}, u32[]{:S(2)}) async-start(bf16[4,2,1024]{2,1,0:T(2,128)(2,1)} %reshape.512), calls=%async_computation.1 | async-start | bytes 32768 | tf_op jit(solution)/shard_map/all_to_all | solution.py:132
where the time goes:
time: 62.1 us; the launch traced here: 61.4 us
  local copies, waits for them, and re-layouts  20.3 us (33%)
  starting transfers between devices  11.4 us (18%)
  matrix products  9.71 us (16%)
  other arithmetic  8.5 us (14%)
  blocking collectives  5.63 us (9%)
  waiting for transfers between devices  4.02 us (6%)
  between operations  1.81 us (3%)
    unnamed x72, local copies, waits for them, and re-layouts  9.6 us
    all_to_all x1, starting transfers between devices, body(): lax.all_to_all(c_dec, 'sample', split_axis=1, concat_axis=0, tiled=True)  6.35 us
    psum x1, blocking collectives, body(): pre_totals = lax.psum(jnp.sum(gated_rows * gated_rows, axis=-1), 'head')  5.63 us
    all_to_all x1, starting transfers between devices, body(): lax.all_to_all(answers.astype(jnp.bfloat16), 'sample', split_axis=0, conc...  5.09 us
    all_to_all x1, waiting for transfers between devices, body(): lax.all_to_all(answers.astype(jnp.bfloat16), 'sample', split_axis=0, conc...  4.01 us
    dot_general x1, matrix products, scan_prompt(): jnp.einsum('cijh,cjhp->cihp', scores, values, precision=highest)  3.96 us
    dot_general x1, matrix products, scan_prompt(): jnp.einsum('cjhn,cjhp->cnhp', b_head * tail_decay[..., None], values, pre...  2.73 us
    dot_general x1, matrix products, scan_prompt(): jnp.einsum('cihn,cnhp->cihp', c_head, starts, precision=highest)  2.2 us
  transfers between devices with their start and end apart: 2, of which 1 were waited for; matrix products, arithmetic and copies ran while one was open for 49% of the time, Pallas kernels for 0%

commit v1 on v0

--- a/solution.py
+++ b/solution.py
@@ -9,6 +9,18 @@
 BLOCK = 128
 epsilon = 1e-05
 highest = lax.Precision.HIGHEST
+
+
+def cut_along(value, dim, length):
+    lengths = value.shape
+    tiles = value.reshape(*lengths[:dim], length, lengths[dim] // length, *lengths[dim + 1 :])
+    return jnp.moveaxis(tiles, dim, 0)
+
+
+def laid_out(tiles, dim):
+    tiles = jnp.moveaxis(tiles, 0, dim)
+    dims = tiles.shape
+    return tiles.reshape(*dims[:dim], dims[dim] * dims[dim + 1], *dims[dim + 2 :])
 
 
 def group_owners(first_head, head_count):
@@ -125,7 +137,15 @@
     prompts_here = final_state.shape[0]
     states = final_state.shape[1]
     cached = final_state.reshape(prompts_here, states, heads_here, head_width)
-    queries = lax.all_to_all(c_dec, "sample", split_axis=1, concat_axis=0, tiled=True)
+    size, index = (lax.axis_size("sample"), lax.axis_index("sample"))
+    parts = cut_along(c_dec, 1, size)
+    filled = parts
+    for step in range(1, size):
+        target, source = ((index + step) % size, (index - step) % size)
+        sent = lax.dynamic_index_in_dim(parts, target, 0)
+        other = lax.ppermute(sent, "sample", [(i, (i + step) % size) for i in range(size)])
+        filled = lax.dynamic_update_slice_in_dim(filled, other, source, axis=0)
+    queries = laid_out(filled, 0)
     c_head = select_heads(queries, owners)
     answers = jnp.einsum("sphn,pnhq->sphq", c_head, cached, preferred_element_type=jnp.float32)
     answers = answers.reshape(answers.shape[0], prompts_here, heads_here * head_width)

time: 62.1 us -> 61.4 us (0.989)
  local copies, waits for them, and re-layouts: 20.3 us -> 22.1 us
  other arithmetic: 8.5 us -> 7.28 us
  starting transfers between devices: 11.4 us -> 10.2 us
    ppermute x0 -> x3, starting transfers between devices: none -> 6.99 us  [body(): lax.ppermute(sent, 'sample', [(i, (i + step) % size) for i in range(size)])]
    all_to_all x1 -> x0, starting transfers between devices: 6.35 us -> none  [body(): lax.all_to_all(c_dec, 'sample', split_axis=1, concat_axis=0, tiled=True)]
    dynamic_update_slice x0 -> x3, local copies, waits for them, and re-layouts: none -> 2.09 us  [body(): filled = lax.dynamic_update_slice_in_dim(filled, other, source, axis=0)]
    unnamed x72 -> x61, local copies, waits for them, and re-layouts: 9.6 us -> 7.65 us
    all_to_all x1, starting transfers between devices: 5.09 us -> 3.25 us  [body(): lax.all_to_all(answers.astype(jnp.bfloat16), 'sample', split_axis=0, conc...]
    mul x1, other arithmetic: 0.71 us -> 1.44 us  [scan_prompt(): b_head * tail_decay[..., None]]
    unnamed x1 -> x0, other arithmetic: 0.67 us -> none
    another operation x1, local copies, waits for them, and re-layouts: 0.05 us -> 0.68 us  [scan_prompt(): decays = jnp.cumsum(-block_delta * rates, axis=1)]
  transfers between devices with their start and end apart: 2 -> 4, of which waited for: 1 -> 1; matrix products, arithmetic and copies ran while one was open for 49% -> 52% of each run, Pallas kernels for 0% -> 0%
where the time goes in v1:
time: 61.4 us; the launch traced here: 60.8 us
  local copies, waits for them, and re-layouts  22.1 us (36%)
  starting transfers between devices  10.2 us (17%)
  matrix products  9.7 us (16%)
  other arithmetic  7.28 us (12%)
  blocking collectives  5.63 us (9%)
  waiting for transfers between devices  3.98 us (6%)
  between operations  1.82 us (3%)
    unnamed x61, local copies, waits for them, and re-layouts  7.65 us
    ppermute x3, starting transfers between devices, body(): lax.ppermute(sent, 'sample', [(i, (i + step) % size) for i in range(size)])  6.99 us
    psum x1, blocking collectives, body(): pre_totals = lax.psum(jnp.sum(gated_rows * gated_rows, axis=-1), 'head')  5.63 us
    all_to_all x1, waiting for transfers between devices, body(): lax.all_to_all(answers.astype(jnp.bfloat16), 'sample', split_axis=0, conc...  3.97 us
    dot_general x1, matrix products, scan_prompt(): jnp.einsum('cijh,cjhp->cihp', scores, values, precision=highest)  3.96 us
    all_to_all x1, starting transfers between devices, body(): lax.all_to_all(answers.astype(jnp.bfloat16), 'sample', split_axis=0, conc...  3.25 us
    dot_general x1, matrix products, scan_prompt(): jnp.einsum('cjhn,cjhp->cnhp', b_head * tail_decay[..., None], values, pre...  2.73 us
    dot_general x1, matrix products, scan_prompt(): jnp.einsum('cihn,cnhp->cihp', c_head, starts, precision=highest)  2.2 us
  transfers between devices with their start and end apart: 4, of which 1 were waited for; matrix products, arithmetic and copies ran while one was open for 52% of the time, Pallas kernels for 0%

profile of v1, /device:TPU:0, one launch (start us, length us, event | category | flops | bytes accessed | tf_op | source)
XLA Modules:
  0.0 60.8 jit_solution(10176095810510432195)
XLA Ops:
  0.7 0.8 %copy.143 = bf16[1,4,512]{2,1,0:T(4,128)(2,1)S(1)} copy(bf16[1,4,512]{2,1,0:T(4,128)(2,1)} %param.32) | data formatting | bytes 8192
  1.4 0.6 dynamic-slice_bitcast_fusion
  2.0 3.1 %collective-permute-start = (bf16[1,1,1,512]{3,0,2,1:T(2,128)(2,1)}, bf16[1,1,1,512]{3,0,2,1:T(2,128)(2,1)}, u32[]{:S(2)}, u32[]{:S(2)}) collective-permute-start(bf16[1,1,1,512]{3,0,2,1:T(2,128)(2,1)} %get-tuple-element.77), channel_id=1, source_target_pairs={{0,4},{4,8},{8,12},{12,0},{1,5},{5,9},{9,13},{13,1},{2,6},{6,10},{... | collective-permute-start | bytes 3080 | tf_op jit(solution)/shard_map/ppermute | solution.py:146
  5.0 2.6 %collective-permute-start.1 = (bf16[1,1,1,512]{3,0,2,1:T(2,128)(2,1)}, bf16[1,1,1,512]{3,0,2,1:T(2,128)(2,1)}, u32[]{:S(2)}, u32[]{:S(2)}) collective-permute-start(bf16[1,1,1,512]{3,0,2,1:T(2,128)(2,1)} %get-tuple-element.76), channel_id=1, source_target_pairs={{0,8},{4,12},{8,0},{12,4},{1,9},{5,13},{9,1},{13,5},{2,10},{6,14},... | collective-permute-start | bytes 3080 | tf_op jit(solution)/shard_map/ppermute | solution.py:146
  7.6 1.3 %collective-permute-start.2 = (bf16[1,1,1,512]{3,0,2,1:T(2,128)(2,1)}, bf16[1,1,1,512]{3,0,2,1:T(2,128)(2,1)}, u32[]{:S(2)}, u32[]{:S(2)}) collective-permute-start(bf16[1,1,1,512]{3,0,2,1:T(2,128)(2,1)} %get-tuple-element.75), channel_id=1, source_target_pairs={{0,12},{4,0},{8,4},{12,8},{1,13},{5,1},{9,5},{13,9},{2,14},{6,2},{... | collective-permute-start | bytes 3080 | tf_op jit(solution)/shard_map/ppermute | solution.py:146
  9.7 0.8 %negate_multiply_fusion = f32[1,128,32]{1,2,0:T(8,128)S(1)} fusion(f32[32]{0:T(128)} %param.25, f32[128]{0:T(128)S(1)} %compare_convert_fusion, f32[1,128,32]{1,2,0:T(8,128)} %param.22, f32[32]{0:T(128)} %param.26), kind=kLoop, calls=%fused_computation.73 | loop fusion | flops 40960 | bytes 33536 | tf_op jit(solution)/shard_map/while/body/eval_jaxpr/mul | solution.py:51
  10.8 0.7 %copy.111 = f32[1,128,32]{1,2,0:T(8,128)} copy(f32[1,128,32]{2,1,0:T(8,128)S(1)} %reduce_window_sum.12) | data formatting | bytes 32768 | tf_op jit(solution)/shard_map/while/body/eval_jaxpr/jit(cumsum)/reduce_window_sum | solution.py:51
  11.4 0.5 slice_bitcast_fusion
  12.0 0.5 compare_and_fusion
  12.5 0.6 %iota_compare_fusion = pred[128,128]{0,1:T(8,128)(4,1)} fusion(), kind=kLoop, calls=%fused_computation.55 | loop fusion | flops 16384 | bytes 16384 | tf_op jit(solution)/shard_map/while/body/eval_jaxpr/ge | solution.py:52
  13.1 0.9 %reshape.435 = bf16[128,4,128]{2,1,0:T(4,128)(2,1)S(1)} reshape(bf16[1,128,512]{2,1,0:T(8,128)(2,1)} %param.21) | data formatting | bytes 262144 | tf_op jit(solution)/shard_map/reshape.21
  14.1 1.0 %copy.102 = bf16[1,128,512]{1,2,0:T(8,128)(2,1)S(1)} copy(bf16[1,128,512]{2,1,0:T(8,128)(2,1)} %param.21) | data formatting | bytes 262144 | tf_op args[3]
  15.1 0.5 compare_select_fusion.3
  15.6 2.0 %copy.100 = bf16[1,128,2048]{1,2,0:T(8,128)(2,1)} copy(bf16[1,128,2048]{2,1,0:T(8,128)(2,1)} %param.18) | data formatting | bytes 1048576 | tf_op args[0]
  17.7 1.2 %copy.106 = f32[1,128,2048]{1,2,0:T(8,128)} copy(bf16[1,128,2048]{2,1,0:T(8,128)(2,1)S(1)} %copy-done.2) | data formatting | bytes 1572864 | tf_op jit(solution)/shard_map/while/body/eval_jaxpr/convert_element_type | solution.py:49
  18.9 0.6 fusion.59
  19.5 0.8 %copy.109 = bf16[1,128,512]{1,2,0:T(8,128)(2,1)} copy(bf16[1,128,512]{2,1,0:T(8,128)(2,1)S(1)} %copy-done.6) | data formatting | bytes 262144 | tf_op args[2]
  20.3 0.7 %copy.98 = f32[128,32]{0,1:T(8,128)} copy(f32[128,32]{1,0:T(8,128)S(1)} %bitcast.137) | data formatting | bytes 32768 | tf_op jit(solution)/shard_map/while/body/eval_jaxpr/sub | solution.py:53
  21.0 0.3 copy.104
  21.5 0.7 %copy.105 = f32[128,32]{0,1:T(8,128)} copy(f32[128,32]{1,0:T(8,128)S(1)} %bitcast_exponential_fusion) | data formatting | bytes 32768 | tf_op jit(solution)/shard_map/while/body/eval_jaxpr/exp | solution.py:74
  22.1 0.2 convolution_bitcast_fusion.1
  22.3 0.7 %gather_fusion = f32[32,128,128]{1,2,0:T(8,128)S(1)} fusion(f32[128,128,4]{0,1,2:T(8,128)S(1)} %convolution_bitcast_fusion.1, s32[1024]{0:T(1024)S(1)} %pad_clamp_fusion.1), kind=kCustom, calls=%fused_computation.2 | custom fusion | bytes 4194432 | tf_op jit(solution)/shard_map/while/body/eval_jaxpr/jit(_take)/gather | solution.py:46
  23.1 1.4 %multiply_bitcast_fusion = (f32[128,32]{0,1:T(8,128)}, f32[128,32]{0,1:T(8,128)S(1)}) fusion(f32[1,128,32]{1,2,0:T(8,128)} %copy.111, f32[32]{0:T(128)} %slice_bitcast_fusion, f32[128]{0:T(128)} %copy-done.16, f32[1,128,32]{1,2,0:T(8,128)} %param.22, f32[32]{0:T(128)} %param.26), kind=kLoop, calls=%fused_computation.72 | loop fusion | flops 40960 | bytes 66304 | tf_op jit(solution)/shard_map/while/body/eval_jaxpr/mul | solution.py:59
  24.5 1.7 %gather_fusion.2 = bf16[32,128,128]{2,1,0:T(8,128)(2,1)} fusion(bf16[128,4,128]{2,0,1:T(8,128)(2,1)S(1)} %bitcast.131, s32[1024]{0:T(1024)S(1)} %pad_clamp_fusion), kind=kCustom, calls=%fused_computation.clone | custom fusion | bytes 2097280 | tf_op jit(solution)/shard_map/while/body/eval_jaxpr/jit(_take)/gather | solution.py:48
  26.2 4.0 %fusion.12 = f32[1,128,32,64]{1,3,2,0:T(8,128)S(1)} fusion(bf16[128,32,64]{0,2,1:T(8,128)(2,1)} %bitcast.141, f32[32,128,128]{1,2,0:T(8,128)S(1)} %gather_fusion, f32[128,32]{0,1:T(8,128)S(1)} %get-tuple-element.74, f32[128,32]{0,1:T(8,128)S(1)} %copy-done.12, pred[32]{0:T(512)(128)(4,1)S(1)} %copy-done.22, pred[128,128]{0,1:T(8,128)(4,1)S(1)} %copy-done.13), kind=kOutput, calls=%fused_computation.16 | convolution fusion | flops 405798912 | bytes 3719200 | tf_op jit(solution)/shard_map/while/body/eval_jaxpr/cijh,cjhp->cihp/dot_general | solution.py:56
  30.2 2.2 %fusion.17 = f32[1,128,32,64]{1,3,2,0:T(8,128)S(1)} fusion(f32[1,128,32,64]{1,3,2,0:T(8,128)S(1)} %fusion.12, f32[128,32,64]{0,2,1:T(8,128)S(1)} %bitcast.133, bf16[32,128,128]{2,1,0:T(8,128)(2,1)S(1)} %copy-done, f32[1,128,32,64]{1,3,2,0:T(8,128)S(1)} %bitcast.134, pred[32]{0:T(512)(128)(4,1)S(1)} %copy-done.22, f32[32]{0:T(128)S(1)} %copy-done.21, ...), kind=kOutput, calls=%fused_computation.20 | convolution fusion | flops 404226048 | bytes 5259424 | tf_op jit(solution)/shard_map/while/body/eval_jaxpr/cihn,cnhp->cihp/dot_general | solution.py:73
  32.5 0.3 copy.107
  32.9 0.3 copy-done.18
  33.6 1.7 %gather_fusion.3 = bf16[32,128,128]{2,1,0:T(8,128)(2,1)} fusion(bf16[128,4,128]{2,0,1:T(8,128)(2,1)S(1)} %bitcast.132, s32[1024]{0:T(1024)S(1)} %pad_clamp_fusion), kind=kCustom, calls=%fused_computation.1.clone | custom fusion | bytes 2097280 | tf_op jit(solution)/shard_map/while/body/eval_jaxpr/jit(_take)/gather | solution.py:47
  35.2 0.4 multiply_reduce_fusion
  35.7 2.7 %fusion = f32[32,128,64]{1,2,0:T(8,128)S(1)} fusion(bf16[128,32,64]{0,2,1:T(8,128)(2,1)S(1)} %bitcast.142, bf16[32,128,128]{2,1,0:T(8,128)(2,1)} %gather_fusion.3, f32[128,32]{0,1:T(8,128)S(1)} %copy-done.14, pred[32]{0:T(512)(128)(4,1)S(1)} %copy-done.23), kind=kOutput, calls=%fused_computation.4 | convolution fusion | flops 404226048 | bytes 2637856 | tf_op jit(solution)/shard_map/while/body/eval_jaxpr/cjhn,cjhp->cnhp/dot_general | solution.py:58
  38.5 0.4 fusion.26
  39.0 0.7 %dynamic_update_slice.18 = bf16[4,1,1,512]{3,0,2,1:T(4,128)(2,1)S(1)} dynamic-update-slice(bf16[4,1,1,512]{3,0,2,1:T(4,128)(2,1)S(1)} %bitcast.139, bf16[1,1,1,512]{3,0,2,1:T(2,128)(2,1)} %collective-permute-done, s32[]{:T(128)S(6)} %select_n.147, s32[]{:T(128)} %constant.154.clone.1, s32[]{:T(128)} %constant.154.clone.1, s32[]{:T(128)} %constant.154.clone.1) | dynamic-update-slice | bytes 2052 | tf_op jit(solution)/shard_map/dynamic_update_slice | solution.py:147
  39.6 0.7 %dynamic_update_slice.19 = bf16[4,1,1,512]{3,0,2,1:T(4,128)(2,1)S(1)} dynamic-update-slice(bf16[4,1,1,512]{3,0,2,1:T(4,128)(2,1)S(1)} %dynamic_update_slice.18, bf16[1,1,1,512]{3,0,2,1:T(2,128)(2,1)} %collective-permute-done.1, s32[]{:T(128)S(6)} %select_n.151, s32[]{:T(128)} %constant.154.clone.1, s32[]{:T(128)} %constant.154.clone.1, s32[]{:T(128)} %constant.154.clone.1) | dynamic-update-slice | bytes 2052 | tf_op jit(solution)/shard_map/dynamic_update_slice | solution.py:147
  40.3 0.7 %dynamic_update_slice.20 = bf16[4,1,1,512]{3,0,2,1:T(4,128)(2,1)S(1)} dynamic-update-slice(bf16[4,1,1,512]{3,0,2,1:T(4,128)(2,1)S(1)} %dynamic_update_slice.19, bf16[1,1,1,512]{3,0,2,1:T(2,128)(2,1)} %collective-permute-done.2, s32[]{:T(128)S(6)} %select_n.155, s32[]{:T(128)} %constant.154.clone.1, s32[]{:T(128)} %constant.154.clone.1, s32[]{:T(128)} %constant.154.clone.1) | dynamic-update-slice | bytes 2052 | tf_op jit(solution)/shard_map/dynamic_update_slice | solution.py:147
  41.1 0.6 gather_fusion.1
  41.7 0.4 fusion.18
  42.2 0.5 broadcast.377
  42.7 0.7 %reduce.4 = bf16[4,2048]{1,0:T(4,128)(2,1)S(1)} reduce(bf16[4,1,2048]{2,1,0:T(2,128)(2,1)S(1)} %convert_element_type.108, bf16[]{:T(256)} %broadcast.377), dimensions={1}, to_apply=%convert_element_type.108.reduce_sub_computation | reduce | bytes 32770 | tf_op jit(solution)/shard_map/convert_element_type | solution.py:153
  43.5 0.6 %reshape.504 = bf16[4,2,1024]{2,1,0:T(2,128)(2,1)} reshape(bf16[4,2048]{1,0:T(4,128)(2,1)S(1)} %reduce.4) | data formatting | bytes 32768
  44.1 3.3 %all-to-all-start = ((bf16[4,2,1024]{2,1,0:T(2,128)(2,1)}), bf16[4,2,1024]{2,1,0:T(2,128)(2,1)S(1)}, u32[]{:S(2)}, u32[]{:S(2)}) async-start(bf16[4,2,1024]{2,1,0:T(2,128)(2,1)} %reshape.504), calls=%async_computation | async-start | bytes 32768 | tf_op jit(solution)/shard_map/all_to_all | solution.py:152
  47.4 0.2 fusion.21
  47.5 1.0 %copy.116 = bf16[1,128,2048]{2,1,0:T(8,128)(2,1)} copy(bf16[1,128,2048]{1,2,0:T(8,128)(2,1)S(1)} %fusion.26) | data formatting | bytes 1048576
  49.0 4.0 %all-to-all-done = bf16[4,2,1024]{2,1,0:T(2,128)(2,1)S(1)} async-done(((bf16[4,2,1024]{2,1,0:T(2,128)(2,1)}), bf16[4,2,1024]{2,1,0:T(2,128)(2,1)S(1)}, u32[]{:S(2)}, u32[]{:S(2)}) %all-to-all-start) | async-done | bytes 16416 | tf_op jit(solution)/shard_map/all_to_all | solution.py:152
  53.0 0.2 multiply_reduce_fusion.1
  53.2 5.6 %all-reduce = (f32[1,128]{1,0:T(1,128)S(1)}, f32[1,4]{1,0:T(1,128)S(1)}) all-reduce(f32[1,128]{1,0:T(1,128)S(1)} %bitcast.145, f32[1,4]{1,0:T(1,128)S(1)} %bitcast.146), channel_id=1, replica_groups=mesh['rep'=2,'sample'=4,'head'=4] {'head'}, use_global_device_ids=true, to_apply=%region_2.4 | all-reduce | flops 132 | bytes 1056 | tf_op jit(solution)/shard_map/psum | solution.py:132
  58.9 1.2 %multiply_convert_fusion = bf16[1,128,2048]{2,1,0:T(8,128)(2,1)} fusion(f32[128]{0:T(128)S(1)} %copy-done.17, f32[2048]{0:T(1024)S(1)} %copy-done.9, f32[128]{0:T(128)S(1)} %rsqrt_bitcast_fusion.1, f32[1,128,2048]{2,1,0:T(8,128)S(1)} %copy.107, bf16[1,128,2048]{2,1,0:T(8,128)(2,1)S(1)} %copy-done.3), kind=kLoop, calls=%fused_computation.41 | loop fusion | flops 2621440 | bytes 2106368 | tf_op jit(solution)/shard_map/convert_element_type | solution.py:134
  60.2 0.6 %copy.117 = bf16[1,4,2048]{2,1,0:T(4,128)(2,1)} copy(bf16[1,4,2048]{2,0,1:T(2,128)(2,1)S(1)} %multiply_convert_fusion.1) | data formatting | bytes 32768
  (80 shorter events, 1.7 us)
Async XLA Ops:
  0.6 17.0 %copy-start.2 = (bf16[1,128,2048]{2,1,0:T(8,128)(2,1)S(1)}, bf16[1,128,2048]{2,1,0:T(8,128)(2,1)}, u32[]{:S(2)}) copy-start(bf16[1,128,2048]{2,1,0:T(8,128)(2,1)} %param.18) | copy-start | bytes 1572868
  0.6 18.8 %copy-start.6 = (bf16[1,128,512]{2,1,0:T(8,128)(2,1)S(1)}, bf16[1,128,512]{2,1,0:T(8,128)(2,1)}, u32[]{:S(2)}) copy-start(bf16[1,128,512]{2,1,0:T(8,128)(2,1)} %param.20) | copy-start | bytes 393220
  2.0 36.9 %collective-permute-start = (bf16[1,1,1,512]{3,0,2,1:T(2,128)(2,1)}, bf16[1,1,1,512]{3,0,2,1:T(2,128)(2,1)}, u32[]{:S(2)}, u32[]{:S(2)}) collective-permute-start(bf16[1,1,1,512]{3,0,2,1:T(2,128)(2,1)} %get-tuple-element.77), channel_id=1, source_target_pairs={{0,4},{4,8},{8,12},{12,0},{1,5},{5,9},{9,13},{13,1},{2,6},{6,10},{... | collective-permute-start | bytes 3080 | tf_op jit(solution)/shard_map/ppermute | solution.py:146
  5.0 34.6 %collective-permute-start.1 = (bf16[1,1,1,512]{3,0,2,1:T(2,128)(2,1)}, bf16[1,1,1,512]{3,0,2,1:T(2,128)(2,1)}, u32[]{:S(2)}, u32[]{:S(2)}) collective-permute-start(bf16[1,1,1,512]{3,0,2,1:T(2,128)(2,1)} %get-tuple-element.76), channel_id=1, source_target_pairs={{0,8},{4,12},{8,0},{12,4},{1,9},{5,13},{9,1},{13,5},{2,10},{6,14},... | collective-permute-start | bytes 3080 | tf_op jit(solution)/shard_map/ppermute | solution.py:146
  7.6 32.7 %collective-permute-start.2 = (bf16[1,1,1,512]{3,0,2,1:T(2,128)(2,1)}, bf16[1,1,1,512]{3,0,2,1:T(2,128)(2,1)}, u32[]{:S(2)}, u32[]{:S(2)}) collective-permute-start(bf16[1,1,1,512]{3,0,2,1:T(2,128)(2,1)} %get-tuple-element.75), channel_id=1, source_target_pairs={{0,12},{4,0},{8,4},{12,8},{1,13},{5,1},{9,5},{13,9},{2,14},{6,2},{... | collective-permute-start | bytes 3080 | tf_op jit(solution)/shard_map/ppermute | solution.py:146
  9.6 0.8 %copy-start.16 = (f32[128]{0:T(128)}, f32[128]{0:T(128)S(1)}, u32[]{:S(2)}) copy-start(f32[128]{0:T(128)S(1)} %compare_convert_fusion) | copy-start | bytes 1540
  10.6 10.4 %copy-start.4 = (f32[1,128,2048]{2,1,0:T(8,128)S(1)}, f32[1,128,2048]{2,1,0:T(8,128)}, u32[]{:S(2)}) copy-start(f32[1,128,2048]{2,1,0:T(8,128)} %param.24) | copy-start | bytes 3145732
  23.0 3.2 %copy-start.12 = (f32[128,32]{0,1:T(8,128)S(1)}, f32[128,32]{0,1:T(8,128)}, u32[]{:S(2)}) copy-start(f32[128,32]{0,1:T(8,128)} %copy.98) | copy-start | bytes 49156
  23.0 3.1 %copy-start.13 = (pred[128,128]{0,1:T(8,128)(4,1)S(1)}, pred[128,128]{0,1:T(8,128)(4,1)}, u32[]{:S(2)}) copy-start(pred[128,128]{0,1:T(8,128)(4,1)} %iota_compare_fusion) | copy-start | bytes 49156
  23.0 3.1 %copy-start.22 = (pred[32]{0:T(512)(128)(4,1)S(1)}, pred[32]{0:T(512)(128)(4,1)}, u32[]{:S(2)}) copy-start(pred[32]{0:T(512)(128)(4,1)} %compare_and_fusion) | copy-start | bytes 100
  26.2 4.0 %copy-start = (bf16[32,128,128]{2,1,0:T(8,128)(2,1)S(1)}, bf16[32,128,128]{2,1,0:T(8,128)(2,1)}, u32[]{:S(2)}) copy-start(bf16[32,128,128]{2,1,0:T(8,128)(2,1)} %gather_fusion.2) | copy-start | bytes 3145732
  26.2 4.0 %copy-start.1 = (f32[1,128,2048]{1,2,0:T(8,128)S(1)}, f32[1,128,2048]{1,2,0:T(8,128)}, u32[]{:S(2)}) copy-start(f32[1,128,2048]{1,2,0:T(8,128)} %copy.106) | copy-start | bytes 3145732
  26.2 4.0 %copy-start.8 = (f32[128,32]{0,1:T(8,128)S(1)}, f32[128,32]{0,1:T(8,128)}, u32[]{:S(2)}) copy-start(f32[128,32]{0,1:T(8,128)} %copy.105) | copy-start | bytes 49156
  26.2 4.0 %copy-start.21 = (f32[32]{0:T(128)S(1)}, f32[32]{0:T(128)}, u32[]{:S(2)}) copy-start(f32[32]{0:T(128)} %param.27) | copy-start | bytes 388
  32.4 0.7 %copy-start.18 = (bf16[1,4,512]{2,1,0:T(4,128)(2,1)S(1)}, bf16[1,4,512]{2,1,0:T(4,128)(2,1)}, u32[]{:S(2)}) copy-start(bf16[1,4,512]{2,1,0:T(4,128)(2,1)} %param.31) | copy-start | bytes 12292
  32.5 0.7 %copy-start.15 = (f32[32]{0:T(128)S(1)}, f32[32]{0:T(128)}, u32[]{:S(2)}) copy-start(f32[32]{0:T(128)} %param.26) | copy-start | bytes 388
  32.5 0.7 %copy-start.19 = (f32[32]{0:T(128)S(1)}, f32[32]{0:T(128)}, u32[]{:S(2)}) copy-start(f32[32]{0:T(128)} %param.25) | copy-start | bytes 388
  32.5 0.7 %copy-start.20 = (f32[1,4,32]{2,1,0:T(4,128)S(1)}, f32[1,4,32]{2,1,0:T(4,128)}, u32[]{:S(2)}) copy-start(f32[1,4,32]{2,1,0:T(4,128)} %param.33) | copy-start | bytes 1540
  32.5 0.7 %copy-start.24 = (f32[32]{0:T(128)S(1)}, f32[32]{0:T(128)}, u32[]{:S(2)}) copy-start(f32[32]{0:T(128)} %fusion.59) | copy-start | bytes 388
  32.5 0.9 %copy-start.7 = (bf16[1,128,512]{1,2,0:T(8,128)(2,1)S(1)}, bf16[1,128,512]{1,2,0:T(8,128)(2,1)}, u32[]{:S(2)}) copy-start(bf16[1,128,512]{1,2,0:T(8,128)(2,1)} %copy.109) | copy-start | bytes 393220
  33.1 2.1 %copy-start.3 = (bf16[1,128,2048]{2,1,0:T(8,128)(2,1)S(1)}, bf16[1,128,2048]{2,1,0:T(8,128)(2,1)}, u32[]{:S(2)}) copy-start(bf16[1,128,2048]{2,1,0:T(8,128)(2,1)} %param.19) | copy-start | bytes 1572868
  33.1 2.6 %copy-start.5 = (bf16[1,128,2048]{1,2,0:T(8,128)(2,1)S(1)}, bf16[1,128,2048]{1,2,0:T(8,128)(2,1)}, u32[]{:S(2)}) copy-start(bf16[1,128,2048]{1,2,0:T(8,128)(2,1)} %copy.100) | copy-start | bytes 1572868
  33.1 2.6 %copy-start.14 = (f32[128,32]{0,1:T(8,128)S(1)}, f32[128,32]{0,1:T(8,128)}, u32[]{:S(2)}) copy-start(f32[128,32]{0,1:T(8,128)} %get-tuple-element.73) | copy-start | bytes 49156
  33.1 2.6 %copy-start.23 = (pred[32]{0:T(512)(128)(4,1)S(1)}, pred[32]{0:T(512)(128)(4,1)}, u32[]{:S(2)}) copy-start(pred[32]{0:T(512)(128)(4,1)} %compare_and_fusion) | copy-start | bytes 100
  38.5 8.9 %copy-start.25 = (s32[32]{0:T(128)S(1)}, s32[32]{0:T(128)}, u32[]{:S(2)}) copy-start(s32[32]{0:T(128)} %get-tuple-element.79) | copy-start | bytes 388
  38.5 14.5 %copy-start.10 = (bf16[1,4,2048]{2,1,0:T(4,128)(2,1)S(1)}, bf16[1,4,2048]{2,1,0:T(4,128)(2,1)}, u32[]{:S(2)}) copy-start(bf16[1,4,2048]{2,1,0:T(4,128)(2,1)} %param.30) | copy-start | bytes 49156
  38.5 14.5 %copy-start.11 = (bf16[1,4,2048]{2,1,0:T(4,128)(2,1)S(1)}, bf16[1,4,2048]{2,1,0:T(4,128)(2,1)}, u32[]{:S(2)}) copy-start(bf16[1,4,2048]{2,1,0:T(4,128)(2,1)} %param.29) | copy-start | bytes 49156
  38.5 20.3 %copy-start.9 = (f32[2048]{0:T(1024)S(1)}, f32[2048]{0:T(1024)}, u32[]{:S(2)}) copy-start(f32[2048]{0:T(1024)} %param.28) | copy-start | bytes 24580
  38.5 20.3 %copy-start.17 = (f32[128]{0:T(128)S(1)}, f32[128]{0:T(128)}, u32[]{:S(2)}) copy-start(f32[128]{0:T(128)} %copy-done.16) | copy-start | bytes 1540
  44.1 8.8 %all-to-all-start = ((bf16[4,2,1024]{2,1,0:T(2,128)(2,1)}), bf16[4,2,1024]{2,1,0:T(2,128)(2,1)S(1)}, u32[]{:S(2)}, u32[]{:S(2)}) async-start(bf16[4,2,1024]{2,1,0:T(2,128)(2,1)} %reshape.504), calls=%async_computation | async-start | bytes 32768 | tf_op jit(solution)/shard_map/all_to_all | solution.py:152
